TPU v7x, 32 devices: a whole 2x2x4 slice. The times are simulated.
32 devices in a mesh: pair: 8 (over z, x), rows: 4 (over y, core).
Axes of the slice: x: 2, y: 2, z: 4, core: 2. Of those that a mesh axis runs over, the one named last changes fastest.
Arguments:
- matrix: float32 [16384, 2048], P('rows', 'pair')
- plan: int32 [3, 8], P(None, 'pair'), may hold values 0 or 1
Outputs:
- rotated: float32 [16384, 2048], P('rows', 'pair')
- offness: float32 [3], replicated
All inputs are finite; a program needn't handle non-finite values. No bound on the sum of `plan` on one device may be relied on, other than what follows from the above.
Results may differ from a plain program's by a relative error of at most 0.00025.
Values sent between devices are 32-bit elements; how exact they have to be, the bound alone decides.
A program may use at most 64 MiB of HBM per device.

v0:
```python
import jax
import jax.numpy as jnp
from jax import lax
from jax.sharding import PartitionSpec as P

ROUNDS = 3


def from_behind(x, axis, by):
    peers = lax.axis_size(axis)
    return lax.ppermute(x, axis, [(i, (i + by) % peers) for i in range(peers)])


def off_total(value):
    return lax.psum(value, "pair")


def pass_on(block):
    return from_behind(block, "pair", 1)


def make_rotation(gram, mean_sq, eye, weights):
    diagonal = jnp.diagonal(gram)
    denom = diagonal[:, None] + diagonal[None, :] + mean_sq
    skew = gram * (weights[None, :] - weights[:, None]) / denom
    square = jnp.dot(skew, skew, precision=lax.Precision.HIGHEST)
    plus = eye + skew
    numer = jnp.dot(plus, plus, precision=lax.Precision.HIGHEST)
    lower = jnp.linalg.cholesky(eye - square)
    return jax.scipy.linalg.cho_solve((lower, True), numer)


def local(matrix, plan):
    width = matrix.shape[1]
    half = width // 2
    pair_count = lax.axis_size("pair")
    ncols_all = width * pair_count
    eye = jnp.eye(width, dtype=jnp.float32)
    weights = jnp.arange(width, dtype=jnp.float32) / jnp.float32(width - 1)
    mean_sq = lax.psum(jnp.sum(matrix * matrix), ("pair", "rows")) / ncols_all
    current = matrix
    values = []
    for step in range(ROUNDS):
        partial_gram = lax.dot_general(
            current,
            current,
            (((0,), (0,)), ((), ())),
            precision=lax.Precision.HIGHEST,
            preferred_element_type=jnp.float32,
        )
        gram = lax.psum(partial_gram, "rows")
        offdiag = gram * (1.0 - eye)
        off_local = jnp.sum(offdiag * offdiag)
        if step == 0:
            total_off = off_total(off_local)
        else:
            total_off = off_total(off_local)
        values.append(jnp.sqrt(total_off / (pair_count * width * (width - 1))) / mean_sq)
        rotation = make_rotation(gram, mean_sq, eye, weights)
        keep_last = plan[step, 0] == 1
        turned = jnp.dot(current, rotation, precision=lax.Precision.HIGHEST)
        first_half = turned[:, :half]
        second_half = turned[:, half:]
        kept = jnp.where(keep_last, second_half, first_half)
        moving = jnp.where(keep_last, first_half, second_half)
        arrived = pass_on(moving)
        current = jnp.concatenate([kept, arrived], axis=1)
    return (current, jnp.stack(values))


def solution(mesh):
    in_specs = (P("rows", "pair"), P(None, "pair"))
    out_specs = (P("rows", "pair"), P())
    return jax.shard_map(local, mesh=mesh, in_specs=in_specs, out_specs=out_specs, check_vma=False)
```

profile of v0, /device:TPU:0, one launch (start us, length us, event | category | flops | bytes accessed | tf_op | source)
XLA Modules:
  0.0 539.2 jit_solution(11518162019927558470)
XLA Ops:
  7.2 10.9 %fusion.76 = f32[256,256]{0,1:T(8,128)} fusion(f32[4096,256]{1,0:T(8,128)} %param.5), kind=kOutput, calls=%fused_computation.150 | convolution fusion | flops 3221225472 | bytes 4456448 | tf_op jit(solution)/shard_map/dot_general | solution.py:44
  22.7 42.5 %psum.50 = f32[]{:T(128)} all-reduce(f32[]{:T(128)} %multiply_reduce_fusion), channel_id=1, replica_groups=mesh['pair'=8,'rows'=4] {'pair','rows'}, use_global_device_ids=true, to_apply=%region_2.0 | all-reduce | flops 1 | bytes 8 | tf_op jit(solution)/shard_map/psum | solution.py:40
  71.0 11.7 %cholesky.172 = f32[128,128]{1,0:T(8,128)S(1)} custom-call(f32[128,128]{1,0:T(8,128)S(1)} %cholesky.270), custom_call_target="Cholesky" | custom-call | tf_op jit(solution)/shard_map/jit(cholesky)/cholesky | solution.py:29
  82.8 9.8 %custom-call.23 = f32[1,128,128]{1,2,0:T(8,128)S(1)} custom-call(f32[1,128,128]{2,1,0:T(8,128)S(1)} %get-tuple-element.81), custom_call_target="InvertDiagBlocksLowerTriangular" | custom-call | tf_op jit(solution)/shard_map/jit(cholesky)/cholesky | solution.py:29
  93.1 11.7 %cholesky.189 = f32[128,128]{1,0:T(8,128)S(1)} custom-call(f32[128,128]{1,0:T(8,128)S(1)} %convolution_subtract_fusion.11), custom_call_target="Cholesky" | custom-call | tf_op jit(solution)/shard_map/jit(cholesky)/cholesky | solution.py:29
  110.9 19.8 %custom-call.24 = f32[2,128,128]{1,2,0:T(8,128)S(1)} custom-call(f32[2,128,128]{2,1,0:T(8,128)S(1)} %get-tuple-element.24), custom_call_target="InvertDiagBlocksLowerTriangular" | custom-call | tf_op jit(solution)/shard_map/jit(_cho_solve)/triangular_solve | solution.py:30
  133.3 8.8 %convolution_bitcast_fusion = f32[4096,256]{0,1:T(8,128)S(1)} fusion(f32[4096,256]{1,0:T(8,128)} %param.5, f32[128,256]{1,0:T(8,128)S(1)} %fusion.47, f32[128,256]{1,0:T(8,128)S(1)} %fusion.46), kind=kOutput, calls=%fused_computation.9 | convolution fusion | flops 3221291008 | bytes 8650752 | tf_op jit(solution)/shard_map/dot_general | solution.py:61
  144.8 47.0 %collective-permute-done = f32[4096,128]{0,1:T(8,128)S(1)} collective-permute-done((f32[4096,128]{0,1:T(8,128)S(1)}, f32[4096,128]{0,1:T(8,128)S(1)}, u32[]{:S(2)}, u32[]{:S(2)}) %collective-permute-start) | collective-permute-done | bytes 2097184 | tf_op jit(solution)/shard_map/ppermute | solution.py:11
  193.1 4.2 fusion.3
  198.2 28.8 %all-reduce.8.cloned.1.call-done = f32[256,256]{0,1:T(8,128)} async-done(((f32[256,256]{0,1:T(8,128)}), f32[256,256]{0,1:T(8,128)}) %all-reduce.8.cloned.1.call-update) | async-done | bytes 262160 | tf_op jit(solution)/shard_map/psum | solution.py:51
  231.4 11.7 %cholesky.206 = f32[128,128]{1,0:T(8,128)S(1)} custom-call(f32[128,128]{1,0:T(8,128)S(1)} %cholesky.273), custom_call_target="Cholesky" | custom-call | tf_op jit(solution)/shard_map/jit(cholesky)/cholesky | solution.py:29
  243.9 9.8 %custom-call.25 = f32[1,128,128]{1,2,0:T(8,128)S(1)} custom-call(f32[1,128,128]{2,1,0:T(8,128)S(1)} %get-tuple-element.77), custom_call_target="InvertDiagBlocksLowerTriangular" | custom-call | tf_op jit(solution)/shard_map/jit(cholesky)/cholesky | solution.py:29
  254.2 11.7 %cholesky.223 = f32[128,128]{1,0:T(8,128)S(1)} custom-call(f32[128,128]{1,0:T(8,128)S(1)} %convolution_subtract_fusion.10), custom_call_target="Cholesky" | custom-call | tf_op jit(solution)/shard_map/jit(cholesky)/cholesky | solution.py:29
  268.0 4.5 while.7
  272.5 19.7 %custom-call.26 = f32[2,128,128]{1,2,0:T(8,128)S(1)} custom-call(f32[2,128,128]{2,1,0:T(8,128)S(1)} %get-tuple-element.25), custom_call_target="InvertDiagBlocksLowerTriangular" | custom-call | tf_op jit(solution)/shard_map/jit(_cho_solve)/triangular_solve | solution.py:30
  300.7 47.2 %collective-permute-done.1 = f32[4096,128]{0,1:T(8,128)S(1)} collective-permute-done((f32[4096,128]{0,1:T(8,128)S(1)}, f32[4096,128]{0,1:T(8,128)S(1)}, u32[]{:S(2)}, u32[]{:S(2)}) %collective-permute-start.1) | collective-permute-done | bytes 2097184 | tf_op jit(solution)/shard_map/ppermute | solution.py:11
  349.3 4.2 fusion.1
  354.1 29.9 %all-reduce.10.cloned.1.call-done = f32[256,256]{0,1:T(8,128)} async-done(((f32[256,256]{0,1:T(8,128)}), f32[256,256]{0,1:T(8,128)}) %all-reduce.10.cloned.1.call-update) | async-done | bytes 262160 | tf_op jit(solution)/shard_map/psum | solution.py:51
  389.1 11.7 %cholesky.240 = f32[128,128]{1,0:T(8,128)S(1)} custom-call(f32[128,128]{1,0:T(8,128)S(1)} %cholesky.276), custom_call_target="Cholesky" | custom-call | tf_op jit(solution)/shard_map/jit(cholesky)/cholesky | solution.py:29
  401.5 9.8 %custom-call.27 = f32[1,128,128]{1,2,0:T(8,128)S(1)} custom-call(f32[1,128,128]{2,1,0:T(8,128)S(1)} %get-tuple-element.73), custom_call_target="InvertDiagBlocksLowerTriangular" | custom-call | tf_op jit(solution)/shard_map/jit(cholesky)/cholesky | solution.py:29
  413.5 11.9 %cholesky.257 = f32[128,128]{1,0:T(8,128)S(1)} custom-call(f32[128,128]{1,0:T(8,128)S(1)} %convolution_subtract_fusion.9), custom_call_target="Cholesky" | custom-call | tf_op jit(solution)/shard_map/jit(cholesky)/cholesky | solution.py:29
  431.2 19.7 %custom-call.28 = f32[2,128,128]{1,2,0:T(8,128)S(1)} custom-call(f32[2,128,128]{2,1,0:T(8,128)S(1)} %get-tuple-element.26), custom_call_target="InvertDiagBlocksLowerTriangular" | custom-call | tf_op jit(solution)/shard_map/jit(_cho_solve)/triangular_solve | solution.py:30
  462.7 57.4 %all-reduce.1 = (f32[]{:T(128)}, f32[]{:T(128)}, f32[]{:T(128)}) all-reduce(f32[]{:T(128)} %fusion.12, f32[]{:T(128)} %fusion.10, f32[]{:T(128)} %fusion.8), channel_id=1, replica_groups=mesh['pair'=8,'rows'=4] {'pair'}, use_global_device_ids=true, to_apply=%region_14.17 | all-reduce | flops 3 | bytes 24 | tf_op jit(solution)/shard_map/psum | solution.py:15
  526.8 5.6 %copy.23 = f32[4096,256]{1,0:T(8,128)} copy(f32[4096,256]{0,1:T(8,128)} %pad_maximum_fusion.2) | data formatting | bytes 8388608
  (127 shorter events, 77.8 us)
Async XLA Ops:
  7.2 59.4 %all-reduce.6.cloned.1.call-start = ((), (), s32[]{:S(2)}) async-start(), calls=%async_computation | async-start | bytes 524288 | tf_op jit(solution)/shard_map/psum | solution.py:51
  18.1 4.0 copy-start.8
  18.1 208.9 %all-reduce.8.cloned.1.call-start = ((), (), s32[]{:S(2)}) async-start(), calls=%async_computation.1 | async-start | bytes 524288 | tf_op jit(solution)/shard_map/psum | solution.py:51
  66.6 64.2 %copy-start = (f32[256,256]{0,1:T(8,128)S(1)}, f32[256,256]{0,1:T(8,128)}, u32[]{:S(2)}) copy-start(f32[256,256]{0,1:T(8,128)} %all-reduce.6.cloned.1.call-done) | copy-start | bytes 786436
  142.5 49.3 %collective-permute-start = (f32[4096,128]{0,1:T(8,128)S(1)}, f32[4096,128]{0,1:T(8,128)S(1)}, u32[]{:S(2)}, u32[]{:S(2)}) collective-permute-start(f32[4096,128]{0,1:T(8,128)S(1)} %get-tuple-element.69), channel_id=1, source_target_pairs={{0,4},{4,8},{8,12},{12,16},{16,20},{20,24},{24,28},{28,0},{1,5},{5... | collective-permute-start | bytes 6291464 | tf_op jit(solution)/shard_map/ppermute | solution.py:11
  191.8 1.3 copy-start.5
  197.3 186.7 %all-reduce.10.cloned.1.call-start = ((), (), s32[]{:S(2)}) async-start(), calls=%async_computation.2 | async-start | bytes 524288 | tf_op jit(solution)/shard_map/psum | solution.py:51
  227.0 65.1 %copy-start.1 = (f32[256,256]{0,1:T(8,128)S(1)}, f32[256,256]{0,1:T(8,128)}, u32[]{:S(2)}) copy-start(f32[256,256]{0,1:T(8,128)} %all-reduce.8.cloned.1.call-done) | copy-start | bytes 786436
  292.1 2.5 copy-start.6
  299.0 48.9 %collective-permute-start.1 = (f32[4096,128]{0,1:T(8,128)S(1)}, f32[4096,128]{0,1:T(8,128)S(1)}, u32[]{:S(2)}, u32[]{:S(2)}) collective-permute-start(f32[4096,128]{0,1:T(8,128)S(1)} %get-tuple-element.67), channel_id=1, source_target_pairs={{0,4},{4,8},{8,12},{12,16},{16,20},{20,24},{24,28},{28,0},{1,5},{5... | collective-permute-start | bytes 6291464 | tf_op jit(solution)/shard_map/ppermute | solution.py:11
  348.0 1.3 copy-start.3
  384.0 66.9 %copy-start.2 = (f32[256,256]{0,1:T(8,128)S(1)}, f32[256,256]{0,1:T(8,128)}, u32[]{:S(2)}) copy-start(f32[256,256]{0,1:T(8,128)} %all-reduce.10.cloned.1.call-done) | copy-start | bytes 786436
  388.4 0.7 copy-start.7
  450.9 2.5 copy-start.4
  459.2 63.7 %collective-permute-start.2 = (f32[4096,128]{0,1:T(8,128)}, f32[4096,128]{0,1:T(8,128)}, u32[]{:S(2)}, u32[]{:S(2)}) collective-permute-start(f32[4096,128]{0,1:T(8,128)} %get-tuple-element.65), channel_id=1, source_target_pairs={{0,4},{4,8},{8,12},{12,16},{16,20},{20,24},{24,28},{28,0},{1,5},{5... | collective-permute-start | bytes 6291464 | tf_op jit(solution)/shard_map/ppermute | solution.py:11
Sparse Core Ops, SparseCore 0:
  18.2 35.0 all-reduce.5
  197.5 29.4 all-reduce.7
  353.7 30.3 all-reduce.9
where the time goes:
time: 546 us; the launch traced here: 539 us
  other arithmetic  176 us (32%)
  waiting for transfers between devices  153 us (28%)
  blocking collectives  100 us (18%)
  matrix products  51.3 us (9%)
  local copies, waits for them, and re-layouts  29.9 us (5%)
  between operations  23 us (4%)
  starting transfers between devices  5.82 us (1%)
    another operation x20, other arithmetic, make_rotation(): lower = jnp.linalg.cholesky(eye - square)  103 us
    ppermute x3, waiting for transfers between devices, from_behind(): return lax.ppermute(x, axis, [(i, (i + by) % peers) for i in range(peers)])  94.2 us
    another operation x7, other arithmetic, make_rotation(): return jax.scipy.linalg.cho_solve((lower, True), numer)  59.3 us
    psum x3, waiting for transfers between devices, local(): gram = lax.psum(partial_gram, 'rows')  58.7 us
    psum x1, blocking collectives, off_total(): return lax.psum(value, 'pair')  57.4 us
    psum x1, blocking collectives, local(): mean_sq = lax.psum(jnp.sum(matrix * matrix), ('pair', 'rows')) / ncols_all  42.5 us
    dot_general x3, matrix products, local(): lax.dot_general(current, current, (((0,), (0,)), ((), ())), precision=lax...  19.4 us
    dot_general x3, matrix products, local(): turned = jnp.dot(current, rotation, precision=lax.Precision.HIGHEST)  16.8 us
  transfers between devices with their start and end apart: 6, of which 4 were waited for; matrix products, arithmetic and copies ran while one was open for 1% of the time, Pallas kernels for 0%

commit v1 on v0

--- a/solution.py
+++ b/solution.py
@@ -48,7 +48,10 @@
             precision=lax.Precision.HIGHEST,
             preferred_element_type=jnp.float32,
         )
-        gram = lax.psum(partial_gram, "rows")
+        size, gram = (lax.axis_size("rows"), partial_gram)
+        for far in [1 << k for k in range(size.bit_length() - 1)]:
+            swap = [(i_2, i_2 ^ far) for i_2 in range(size)]
+            gram = gram + lax.ppermute(gram, "rows", swap)
         offdiag = gram * (1.0 - eye)
         off_local = jnp.sum(offdiag * offdiag)
         if step == 0:

time: 546 us -> 487 us (0.89)
  waiting for transfers between devices: 153 us -> 112 us
  between operations: 23 us -> 9.8 us
    psum x3 -> x0, waiting for transfers between devices: 58.7 us -> none  [local(): gram = lax.psum(partial_gram, 'rows')]
    ppermute x0 -> x6, waiting for transfers between devices: none -> 15.8 us  [local(): gram = gram + lax.ppermute(gram, 'rows', swap)]
    ppermute x0 -> x6, starting transfers between devices: none -> 6.05 us  [local(): gram = gram + lax.ppermute(gram, 'rows', swap)]
  transfers between devices with their start and end apart: 6 -> 9, of which waited for: 4 -> 6; matrix products, arithmetic and copies ran while one was open for 1% -> 1% of each run, Pallas kernels for 0% -> 0%
where the time goes in v1:
time: 487 us; the launch traced here: 482 us
  other arithmetic  173 us (36%)
  waiting for transfers between devices  112 us (23%)
  blocking collectives  102 us (21%)
  matrix products  48.2 us (10%)
  local copies, waits for them, and re-layouts  27.6 us (6%)
  between operations  9.8 us (2%)
  starting transfers between devices  8.44 us (2%)
    another operation x20, other arithmetic, make_rotation(): lower = jnp.linalg.cholesky(eye - square)  103 us
    ppermute x3, waiting for transfers between devices, from_behind(): return lax.ppermute(x, axis, [(i, (i + by) % peers) for i in range(peers)])  96.7 us
    psum x1, blocking collectives, off_total(): return lax.psum(value, 'pair')  59.8 us
    another operation x7, other arithmetic, make_rotation(): return jax.scipy.linalg.cho_solve((lower, True), numer)  59.3 us
    psum x1, blocking collectives, local(): mean_sq = lax.psum(jnp.sum(matrix * matrix), ('pair', 'rows')) / ncols_all  41.7 us
    dot_general x3, matrix products, local(): turned = jnp.dot(current, rotation, precision=lax.Precision.HIGHEST)  20 us
    dot_general x3, matrix products, local(): lax.dot_general(current, current, (((0,), (0,)), ((), ())), precision=lax...  17.7 us
    ppermute x6, waiting for transfers between devices, local(): gram = gram + lax.ppermute(gram, 'rows', swap)  15.8 us
  transfers between devices with their start and end apart: 9, of which 6 were waited for; matrix products, arithmetic and copies ran while one was open for 1% of the time, Pallas kernels for 0%

profile of v1, /device:TPU:0, one launch (start us, length us, event | category | flops | bytes accessed | tf_op | source)
XLA Modules:
  0.0 482.1 jit_solution(10297228630206261997)
XLA Ops:
  0.7 10.7 %fusion.76 = f32[256,256]{0,1:T(8,128)S(1)} fusion(f32[4096,256]{1,0:T(8,128)} %param.5), kind=kOutput, calls=%fused_computation.150 | convolution fusion | flops 3221225472 | bytes 4456448 | tf_op jit(solution)/shard_map/dot_general | solution.py:44
  16.9 41.7 %psum.28 = f32[]{:T(128)} all-reduce(f32[]{:T(128)} %multiply_reduce_fusion), channel_id=1, replica_groups=mesh['pair'=8,'rows'=4] {'pair','rows'}, use_global_device_ids=true, to_apply=%region_1.0 | all-reduce | flops 1 | bytes 8 | tf_op jit(solution)/shard_map/psum | solution.py:40
  64.9 11.7 %cholesky.172 = f32[128,128]{1,0:T(8,128)S(1)} custom-call(f32[128,128]{1,0:T(8,128)S(1)} %cholesky.270), custom_call_target="Cholesky" | custom-call | tf_op jit(solution)/shard_map/jit(cholesky)/cholesky | solution.py:29
  76.6 9.8 %custom-call.23 = f32[1,128,128]{1,2,0:T(8,128)S(1)} custom-call(f32[1,128,128]{2,1,0:T(8,128)S(1)} %get-tuple-element.87), custom_call_target="InvertDiagBlocksLowerTriangular" | custom-call | tf_op jit(solution)/shard_map/jit(cholesky)/cholesky | solution.py:29
  86.9 11.7 %cholesky.189 = f32[128,128]{1,0:T(8,128)S(1)} custom-call(f32[128,128]{1,0:T(8,128)S(1)} %convolution_subtract_fusion.11), custom_call_target="Cholesky" | custom-call | tf_op jit(solution)/shard_map/jit(cholesky)/cholesky | solution.py:29
  104.6 19.8 %custom-call.24 = f32[2,128,128]{1,2,0:T(8,128)S(1)} custom-call(f32[2,128,128]{2,1,0:T(8,128)S(1)} %get-tuple-element.24), custom_call_target="InvertDiagBlocksLowerTriangular" | custom-call | tf_op jit(solution)/shard_map/jit(_cho_solve)/triangular_solve | solution.py:30
  126.3 8.8 %convolution_bitcast_fusion = f32[4096,256]{0,1:T(8,128)S(1)} fusion(f32[4096,256]{1,0:T(8,128)} %param.5, f32[128,256]{1,0:T(8,128)S(1)} %fusion.47, f32[128,256]{1,0:T(8,128)S(1)} %fusion.46), kind=kOutput, calls=%fused_computation.9 | convolution fusion | flops 3221291008 | bytes 8650752 | tf_op jit(solution)/shard_map/dot_general | solution.py:64
  137.7 47.2 %collective-permute-done.2 = f32[4096,128]{0,1:T(8,128)S(1)} collective-permute-done((f32[4096,128]{0,1:T(8,128)S(1)}, f32[4096,128]{0,1:T(8,128)S(1)}, u32[]{:S(2)}, u32[]{:S(2)}) %collective-permute-start.2) | collective-permute-done | bytes 2097184 | tf_op jit(solution)/shard_map/ppermute | solution.py:11
  193.5 6.3 %collective-permute-done.4 = f32[256,256]{0,1:T(8,128)S(1)} collective-permute-done((f32[256,256]{0,1:T(8,128)S(1)}, f32[256,256]{0,1:T(8,128)S(1)}, u32[]{:S(2)}, u32[]{:S(2)}) %collective-permute-start.4) | collective-permute-done | bytes 262176 | tf_op jit(solution)/shard_map/ppermute | solution.py:54
  204.7 11.7 %cholesky.206 = f32[128,128]{1,0:T(8,128)S(1)} custom-call(f32[128,128]{1,0:T(8,128)S(1)} %cholesky.273), custom_call_target="Cholesky" | custom-call | tf_op jit(solution)/shard_map/jit(cholesky)/cholesky | solution.py:29
  216.4 9.8 %custom-call.25 = f32[1,128,128]{1,2,0:T(8,128)S(1)} custom-call(f32[1,128,128]{2,1,0:T(8,128)S(1)} %get-tuple-element.83), custom_call_target="InvertDiagBlocksLowerTriangular" | custom-call | tf_op jit(solution)/shard_map/jit(cholesky)/cholesky | solution.py:29
  226.7 11.7 %cholesky.223 = f32[128,128]{1,0:T(8,128)S(1)} custom-call(f32[128,128]{1,0:T(8,128)S(1)} %convolution_subtract_fusion.10), custom_call_target="Cholesky" | custom-call | tf_op jit(solution)/shard_map/jit(cholesky)/cholesky | solution.py:29
  241.0 4.2 while.7
  245.2 19.7 %custom-call.26 = f32[2,128,128]{1,2,0:T(8,128)S(1)} custom-call(f32[2,128,128]{2,1,0:T(8,128)S(1)} %get-tuple-element.25), custom_call_target="InvertDiagBlocksLowerTriangular" | custom-call | tf_op jit(solution)/shard_map/jit(_cho_solve)/triangular_solve | solution.py:30
  266.6 5.6 %fusion.2 = f32[4096,256]{0,1:T(8,128)S(1)} fusion(f32[4096,128]{0,1:T(8,128)} %copy-done.2, f32[4096,128]{0,1:T(8,128)S(1)} %get-tuple-element.74, f32[128,256]{1,0:T(8,128)S(1)} %fusion.50, f32[128,256]{1,0:T(8,128)S(1)} %fusion.49), kind=kOutput, calls=%fused_computation.16 | convolution fusion | flops 3222339584 | bytes 8650752 | tf_op jit(solution)/shard_map/dot_general | solution.py:64
  272.7 49.5 %collective-permute-done.5 = f32[4096,128]{0,1:T(8,128)S(1)} collective-permute-done((f32[4096,128]{0,1:T(8,128)S(1)}, f32[4096,128]{0,1:T(8,128)S(1)}, u32[]{:S(2)}, u32[]{:S(2)}) %collective-permute-start.5) | collective-permute-done | bytes 2097184 | tf_op jit(solution)/shard_map/ppermute | solution.py:11
  329.4 6.4 %collective-permute-done.7 = f32[256,256]{0,1:T(8,128)S(1)} collective-permute-done((f32[256,256]{0,1:T(8,128)S(1)}, f32[256,256]{0,1:T(8,128)S(1)}, u32[]{:S(2)}, u32[]{:S(2)}) %collective-permute-start.7) | collective-permute-done | bytes 262176 | tf_op jit(solution)/shard_map/ppermute | solution.py:54
  340.5 11.7 %cholesky.240 = f32[128,128]{1,0:T(8,128)S(1)} custom-call(f32[128,128]{1,0:T(8,128)S(1)} %cholesky.276), custom_call_target="Cholesky" | custom-call | tf_op jit(solution)/shard_map/jit(cholesky)/cholesky | solution.py:29
  352.3 9.8 %custom-call.27 = f32[1,128,128]{1,2,0:T(8,128)S(1)} custom-call(f32[1,128,128]{2,1,0:T(8,128)S(1)} %get-tuple-element.79), custom_call_target="InvertDiagBlocksLowerTriangular" | custom-call | tf_op jit(solution)/shard_map/jit(cholesky)/cholesky | solution.py:29
  362.6 11.7 %cholesky.257 = f32[128,128]{1,0:T(8,128)S(1)} custom-call(f32[128,128]{1,0:T(8,128)S(1)} %convolution_subtract_fusion.9), custom_call_target="Cholesky" | custom-call | tf_op jit(solution)/shard_map/jit(cholesky)/cholesky | solution.py:29
  381.1 19.7 %custom-call.28 = f32[2,128,128]{1,2,0:T(8,128)S(1)} custom-call(f32[2,128,128]{2,1,0:T(8,128)S(1)} %get-tuple-element.26), custom_call_target="InvertDiagBlocksLowerTriangular" | custom-call | tf_op jit(solution)/shard_map/jit(_cho_solve)/triangular_solve | solution.py:30
  402.5 5.6 %fusion = f32[4096,256]{0,1:T(8,128)S(1)} fusion(f32[4096,128]{0,1:T(8,128)} %copy-done.1, f32[4096,128]{0,1:T(8,128)S(1)} %get-tuple-element.72, f32[128,256]{1,0:T(8,128)S(1)} %fusion.53, f32[128,256]{1,0:T(8,128)S(1)} %fusion.52), kind=kOutput, calls=%fused_computation.14 | convolution fusion | flops 3222339584 | bytes 8650752 | tf_op jit(solution)/shard_map/dot_general | solution.py:64
  409.9 59.8 %all-reduce.1 = (f32[]{:T(128)}, f32[]{:T(128)}, f32[]{:T(128)}) all-reduce(f32[]{:T(128)} %get-tuple-element.62, f32[]{:T(128)} %get-tuple-element.60, f32[]{:T(128)} %get-tuple-element.58), channel_id=1, replica_groups=mesh['pair'=8,'rows'=4] {'pair'}, use_global_device_ids=true, to_apply=%region_11.14 | all-reduce | flops 3 | bytes 24 | tf_op jit(solution)/shard_map/psum | solution.py:15
  476.3 5.6 %copy.29 = f32[4096,256]{1,0:T(8,128)} copy(f32[4096,256]{0,1:T(8,128)} %pad_maximum_fusion.2) | data formatting | bytes 8388608
  (123 shorter events, 73.5 us)
Async XLA Ops:
  0.6 11.9 %copy-start = (f32[4096,256]{1,0:T(8,128)S(1)}, f32[4096,256]{1,0:T(8,128)}, u32[]{:S(2)}) copy-start(f32[4096,256]{1,0:T(8,128)} %param.5) | copy-start | bytes 12582916
  0.6 11.3 %copy-start.3 = (s32[3,1]{0,1:T(1,128)S(1)}, s32[3,1]{0,1:T(1,128)}, u32[]{:S(2)}) copy-start(s32[3,1]{0,1:T(1,128)} %param.6) | copy-start | bytes 40
  11.3 2.9 collective-permute-start
  14.3 45.5 %collective-permute-start.1 = (f32[256,256]{0,1:T(8,128)S(1)}, f32[256,256]{0,1:T(8,128)S(1)}, u32[]{:S(2)}, u32[]{:S(2)}) collective-permute-start(f32[256,256]{0,1:T(8,128)S(1)} %add.116), channel_id=1, source_target_pairs={{0,2},{1,3},{2,0},{3,1},{4,6},{5,7},{6,4},{7,5},{8,10},{9,11},{10,... | collective-permute-start | bytes 786440 | tf_op jit(solution)/shard_map/ppermute | solution.py:54
  135.4 49.5 %collective-permute-start.2 = (f32[4096,128]{0,1:T(8,128)S(1)}, f32[4096,128]{0,1:T(8,128)S(1)}, u32[]{:S(2)}, u32[]{:S(2)}) collective-permute-start(f32[4096,128]{0,1:T(8,128)S(1)} %get-tuple-element.75), channel_id=1, source_target_pairs={{0,4},{4,8},{8,12},{12,16},{16,20},{20,24},{24,28},{28,0},{1,5},{5... | collective-permute-start | bytes 6291464 | tf_op jit(solution)/shard_map/ppermute | solution.py:11
  184.9 1.3 copy-start.2
  189.8 1.6 collective-permute-start.3
  191.4 8.4 %collective-permute-start.4 = (f32[256,256]{0,1:T(8,128)S(1)}, f32[256,256]{0,1:T(8,128)S(1)}, u32[]{:S(2)}, u32[]{:S(2)}) collective-permute-start(f32[256,256]{0,1:T(8,128)S(1)} %add.124), channel_id=1, source_target_pairs={{0,2},{1,3},{2,0},{3,1},{4,6},{5,7},{6,4},{7,5},{8,10},{9,11},{10,... | collective-permute-start | bytes 786440 | tf_op jit(solution)/shard_map/ppermute | solution.py:54
  272.6 49.6 %collective-permute-start.5 = (f32[4096,128]{0,1:T(8,128)S(1)}, f32[4096,128]{0,1:T(8,128)S(1)}, u32[]{:S(2)}, u32[]{:S(2)}) collective-permute-start(f32[4096,128]{0,1:T(8,128)S(1)} %get-tuple-element.73), channel_id=1, source_target_pairs={{0,4},{4,8},{8,12},{12,16},{16,20},{20,24},{24,28},{28,0},{1,5},{5... | collective-permute-start | bytes 6291464 | tf_op jit(solution)/shard_map/ppermute | solution.py:11
  322.2 7.2 %copy-start.1 = (f32[4096,128]{0,1:T(8,128)}, f32[4096,128]{0,1:T(8,128)S(1)}, u32[]{:S(2)}) copy-start(f32[4096,128]{0,1:T(8,128)S(1)} %collective-permute-done.5) | copy-start | bytes 6291460
  325.7 1.6 collective-permute-start.6
  327.4 8.4 %collective-permute-start.7 = (f32[256,256]{0,1:T(8,128)S(1)}, f32[256,256]{0,1:T(8,128)S(1)}, u32[]{:S(2)}, u32[]{:S(2)}) collective-permute-start(f32[256,256]{0,1:T(8,128)S(1)} %add.131), channel_id=1, source_target_pairs={{0,2},{1,3},{2,0},{3,1},{4,6},{5,7},{6,4},{7,5},{8,10},{9,11},{10,... | collective-permute-start | bytes 786440 | tf_op jit(solution)/shard_map/ppermute | solution.py:54
  409.9 62.5 %collective-permute-start.8 = (f32[4096,128]{0,1:T(8,128)}, f32[4096,128]{0,1:T(8,128)}, u32[]{:S(2)}, u32[]{:S(2)}) collective-permute-start(f32[4096,128]{0,1:T(8,128)} %get-tuple-element.71), channel_id=1, source_target_pairs={{0,4},{4,8},{8,12},{12,16},{16,20},{20,24},{24,28},{28,0},{1,5},{5... | collective-permute-start | bytes 6291464 | tf_op jit(solution)/shard_map/ppermute | solution.py:11
